TPU v7x, 32 devices: a whole 2x2x4 slice. The times are simulated.
32 devices in a mesh: rows: 16 (over z, x, core), split: 2 (over y).
Axes of the slice: x: 2, y: 2, z: 4, core: 2. Of those that a mesh axis runs over, the one named last changes fastest.
Arguments:
- embeddings: bfloat16 [8192, 768], P(('rows', 'split')), may hold values from -24 to 24
- cluster_id: int32 [8192], P(('rows', 'split')), may hold values from 0 to 127, as said below
- owner_map: int32 [128], replicated, may hold values from 0 to 15, as said below
Outputs:
- prune_score: float32 [8192], P(('rows', 'split'))
Inputs may be any that keep to these rules, and one draw needn't show every extreme that they name: `owner_map`: every group 0 to 15 holds exactly 8 clusters. `cluster_id`: within each aligned block of 256 rows (the rows of one device), no group holds more than 32 of the block's rows, and one group holds exactly 32; every group holds exactly 32 rows of some block. Every cluster holds two rows or more.
All inputs are finite; a program needn't handle non-finite values.
Results may differ from a plain program's by a relative error of at most 0.0005.
Values may be sent and summed in bfloat16 or wider, within the bound.
A program may use at most 64 MiB of HBM per device.

v0:
```python
import jax
import jax.numpy as jnp
from jax import lax
from jax.sharding import PartitionSpec as P

FLOOR_SCORE = -1e30


def block_logsumexp(queries, key_rows, allowed):
    score_scale = 1.0 / queries.shape[1] ** 0.5
    scores = (
        jnp.einsum("qd,kd->qk", queries, key_rows, preferred_element_type=jnp.float32) * score_scale
    )
    masked = jnp.where(allowed, scores, FLOOR_SCORE)
    highest = jnp.max(masked, axis=1)
    totals = jnp.sum(jnp.where(allowed, jnp.exp(masked - highest[:, None]), 0.0), axis=1)
    return (highest, totals)


def merge_pair(earlier_pair, later_pair):
    highest = jnp.maximum(earlier_pair[0], later_pair[0])
    totals = later_pair[1] * jnp.exp(later_pair[0] - highest)
    return (highest, totals)


def cluster_means(density, member_ids, clusters_all):
    present = member_ids >= 0
    segment = jnp.where(present, member_ids, clusters_all)
    sum_density = jax.ops.segment_sum(jnp.where(present, density, 0.0), segment, clusters_all + 1)[
        :clusters_all
    ]
    counts = jax.ops.segment_sum(present.astype(jnp.float32), segment, clusters_all + 1)[
        :clusters_all
    ]
    return (sum_density, counts)


def on_device(embeddings, cluster_id, owner_map):
    rows_here = embeddings.shape[0]
    width = embeddings.shape[1]
    clusters_all = owner_map.shape[0]
    owners_count = lax.axis_size("rows")
    capacity = 2 * rows_here // owners_count
    slot_count = owners_count * capacity
    cluster_range = jnp.arange(clusters_all, dtype=jnp.int32)
    table_hit = cluster_id[:, None] == cluster_range[None, :]
    owner_of = jnp.sum(jnp.where(table_hit, owner_map[None, :], 0), axis=1)
    same_owner = owner_of[:, None] == owner_of[None, :]
    earlier = jnp.arange(rows_here)[None, :] < jnp.arange(rows_here)[:, None]
    ranking = jnp.sum(same_owner & earlier, axis=1)
    slot_index = owner_of * capacity + ranking
    placed = jnp.arange(slot_count, dtype=jnp.int32)[:, None] == slot_index[None, :]
    outgoing = jnp.dot(
        placed.astype(jnp.bfloat16), embeddings, preferred_element_type=jnp.float32
    ).astype(jnp.bfloat16)
    out_ids = jnp.sum(jnp.where(placed, cluster_id[None, :] + 1, 0), axis=1) - 1
    arrived, arrived_ids = (
        lax.all_to_all(
            outgoing.reshape(owners_count, capacity, width),
            "rows",
            split_axis=0,
            concat_axis=0,
            tiled=True,
        ),
        lax.all_to_all(
            out_ids.reshape(owners_count, capacity), "rows", split_axis=0, concat_axis=0, tiled=True
        ),
    )
    key_rows = arrived.reshape(slot_count, width)
    key_ids = arrived_ids.reshape(slot_count)
    piece_index = lax.axis_index("split")
    my_start = piece_index * slot_count
    positions = my_start + jnp.arange(slot_count, dtype=jnp.int32)
    initial = (
        jnp.full((slot_count,), FLOOR_SCORE, jnp.float32),
        jnp.zeros((slot_count,), jnp.float32),
    )
    portion_rows = lax.all_gather(key_rows, "split", axis=0, tiled=True)
    portion_ids = lax.all_gather(key_ids, "split", axis=0, tiled=True)
    length = portion_ids.shape[0]
    key_positions = jnp.arange(length, dtype=jnp.int32)
    allowed = (
        (portion_ids[None, :] >= 0)
        & (portion_ids[None, :] == key_ids[:, None])
        & (positions[:, None] != key_positions[None, :])
    )
    highest, totals = merge_pair(initial, block_logsumexp(key_rows, portion_rows, allowed))
    density = highest + jnp.log(totals)
    sum_density, counts = cluster_means(density, key_ids, clusters_all)
    sum_density, counts = lax.psum((sum_density, counts), "split")
    cluster_mean = sum_density / jnp.maximum(counts, 1.0)
    row_hit = key_ids[:, None] == cluster_range[None, :]
    row_mean = jnp.sum(jnp.where(row_hit, cluster_mean[None, :], 0.0), axis=1)
    slot_score = jnp.where(key_ids >= 0, density - row_mean, 0.0)
    returned = lax.all_to_all(
        slot_score.reshape(owners_count, capacity), "rows", split_axis=0, concat_axis=0, tiled=True
    )
    returned_flat = returned.reshape(slot_count)
    return jnp.sum(jnp.where(placed, returned_flat[:, None], 0.0), axis=0)


def solution(mesh):
    placed = (P(("rows", "split"), None), P(("rows", "split")), P())
    return jax.shard_map(
        on_device, mesh=mesh, in_specs=placed, out_specs=P(("rows", "split")), check_vma=False
    )
```

profile of v0, /device:TPU:0, one launch (start us, length us, event | category | flops | bytes accessed | tf_op | source)
XLA Modules:
  0.0 97.4 jit_solution(236340904709516073)
XLA Ops:
  6.5 0.0 copy-start
  6.5 0.0 all-gather.3.cloned.1.call-start
  6.5 0.9 select_reduce_fusion.4
  7.5 0.2 convert_reduce_fusion
  7.6 0.7 multiply_add_fusion
  8.3 0.0 copy-done
  8.3 0.4 convolution_convert_fusion
  8.7 27.4 %all_to_all.17 = bf16[16,32,768]{2,1,0:T(8,128)(2,1)} all-to-all(bf16[16,32,768]{2,1,0:T(8,128)(2,1)S(1)} %bitcast.10), channel_id=1, replica_groups=mesh['rows'=16,'split'=2] {'rows'}, dimensions={0} | all-to-all | bytes 1572864 | tf_op jit(solution)/shard_map/all_to_all | solution.py:58
  36.1 0.0 all-gather.3.cloned.1.call-update
  36.2 0.1 select_reduce_fusion.2
  36.3 0.7 sub.39
  37.0 3.9 %all-to-all-start = ((s32[16,1,32]{2,1,0:T(1,128)}), s32[16,1,32]{2,1,0:T(1,128)S(1)}, u32[]{:S(2)}, u32[]{:S(2)}) async-start(s32[16,1,32]{2,1,0:T(1,128)} %sub.39), calls=%async_computation | async-start | bytes 16384 | tf_op jit(solution)/shard_map/all_to_all | solution.py:65
  41.0 6.4 %all-to-all-done = s32[16,1,32]{2,1,0:T(1,128)S(1)} async-done(((s32[16,1,32]{2,1,0:T(1,128)}), s32[16,1,32]{2,1,0:T(1,128)S(1)}, u32[]{:S(2)}, u32[]{:S(2)}) %all-to-all-start) | async-done | bytes 2080 | tf_op jit(solution)/shard_map/all_to_all | solution.py:65
  47.4 0.1 reshape.127
  47.5 0.1 reshape.130
  47.5 0.5 broadcast.91
  48.0 0.7 reduce.10
  48.7 0.1 reshape.147
  48.8 4.1 %scatter_custom_fusion.1 = f32[129]{0:T(256)S(1)} fusion(s32[512]{0:T(512)S(1)} %bitcast.16, f32[512]{0:T(512)S(1)} %get-tuple-element.7, f32[]{:T(128)} %constant.6.clone.1), kind=kCustom, calls=%fused_computation.38 | custom fusion | flops 512 | bytes 520 | tf_op jit(solution)/shard_map/scatter-add | solution.py:32
  52.9 0.0 copy-start.1
  52.9 4.5 %all-gather = s32[2,1,512]{2,1,0:T(1,128)S(1)} all-gather(s32[1,1,512]{2,1,0:T(1,128)S(1)} %reshape.147), channel_id=1, replica_groups=mesh['rows'=16,'split'=2] {'split'}, dimensions={0}, use_global_device_ids=true | all-gather | bytes 6144 | tf_op jit(solution)/shard_map/all_gather | solution.py:79
  57.5 5.4 %all-gather.3.cloned.1.call-done = bf16[1024,768]{1,0:T(8,128)(2,1)} async-done(((bf16[512,768]{1,0:T(8,128)(2,1)}), bf16[1024,768]{1,0:T(8,128)(2,1)}) %all-gather.3.cloned.1.call-update) | async-done | bytes 1572880 | tf_op jit(solution)/shard_map/all_gather | solution.py:78
  62.9 3.1 %fusion.1 = (f32[512]{0:T(512)S(1)}, f32[512,1024]{1,0:T(8,128)S(1)}) fusion(s32[512]{0:T(512)S(1)} %iota_add_fusion, s32[1024]{0:T(1024)S(1)} %bitcast.14, s32[512]{0:T(512)S(1)} %reshape.127, pred[1024]{0:T(1024)(128)(4,1)S(1)} %broadcast_compare_fusion, bf16[512,768]{1,0:T(8,128)(2,1)} %bitcast.9, bf16[1024,768]{1,0:T(8,128)(2,1)} %all-gather.3.cloned.1.call-done), kind=kOutput, calls=%fused_computation.6 | convolution fusion | flops 808975872 | bytes 4467712 | tf_op jit(solution)/shard_map/qd,kd->qk/dot_general | solution.py:12
  65.9 0.0 copy-done.1
  65.9 0.0 slice-start
  65.9 0.1 reduce_max.12
  66.0 1.2 %select_reduce_fusion = f32[512]{0:T(512)S(1)} fusion(f32[512,1024]{1,0:T(8,128)S(1)} %get-tuple-element.10, f32[512]{0:T(512)S(1)} %get-tuple-element.9, s32[512]{0:T(512)S(1)} %iota_add_fusion, s32[1024]{0:T(1024)S(1)} %bitcast.15, s32[512]{0:T(512)S(1)} %reshape.127, pred[1024]{0:T(1024)(128)(4,1)S(1)} %broadcast_compare_fusion), kind=kLoop, calls=%fused_computation.2 | loop fusion | flops 4718080 | bytes 2110464 | tf_op jit(solution)/shard_map/reduce_sum | solution.py:16
  67.2 0.1 reduce_sum.62
  67.3 4.1 %scatter_custom_fusion = f32[129]{0:T(256)S(1)} fusion(s32[512]{0:T(512)S(1)} %bitcast.17, f32[512]{0:T(512)S(1)} %fusion.10, f32[]{:T(128)} %constant.6.clone.1), kind=kCustom, calls=%fused_computation.40 | custom fusion | flops 512 | bytes 520 | tf_op jit(solution)/shard_map/scatter-add | solution.py:29
  71.4 0.0 slice-done
  71.4 4.9 %all-reduce = (f32[128]{0:T(128)S(1)}, f32[128]{0:T(128)S(1)}) all-reduce(f32[128]{0:T(128)S(1)} %slice.6, f32[128]{0:T(128)S(1)} %slice-done), channel_id=1, replica_groups=mesh['rows'=16,'split'=2] {'split'}, use_global_device_ids=true, to_apply=%region_6.7 | all-reduce | flops 256 | bytes 2048 | tf_op jit(solution)/shard_map/psum | solution.py:90
  76.4 0.2 select_reduce_fusion.3
  76.6 0.1 reduce_sum.64
  76.7 11.9 %all_to_all.18 = f32[16,1,32]{2,1,0:T(1,128)S(1)} all-to-all(f32[16,1,32]{2,1,0:T(1,128)S(1)} %compare_select_fusion), channel_id=1, replica_groups=mesh['rows'=16,'split'=2] {'rows'}, dimensions={0} | all-to-all | bytes 4096 | tf_op jit(solution)/shard_map/all_to_all | solution.py:95
  88.6 0.5 broadcast.92
  89.1 0.7 reduce.11
  89.8 0.1 broadcast_in_dim.105
  89.9 0.7 select_reduce_fusion.1
  (9 shorter events, 0.1 us)
Async XLA Ops:
  6.5 1.8 %copy-start = (bf16[256,768]{1,0:T(8,128)(2,1)S(1)}, bf16[256,768]{1,0:T(8,128)(2,1)}, u32[]{:S(2)}) copy-start(bf16[256,768]{1,0:T(8,128)(2,1)} %param.3) | copy-start | bytes 1179652
  6.5 56.3 %all-gather.3.cloned.1.call-start = ((), (), s32[]{:S(2)}) async-start(), calls=%async_computation.3 | async-start | bytes 2359296 | tf_op jit(solution)/shard_map/all_gather | solution.py:78
  37.0 10.4 %all-to-all-start = ((s32[16,1,32]{2,1,0:T(1,128)}), s32[16,1,32]{2,1,0:T(1,128)S(1)}, u32[]{:S(2)}, u32[]{:S(2)}) async-start(s32[16,1,32]{2,1,0:T(1,128)} %sub.39), calls=%async_computation | async-start | bytes 16384 | tf_op jit(solution)/shard_map/all_to_all | solution.py:65
  52.9 13.0 %copy-start.1 = (f32[129]{0:T(256)}, f32[129]{0:T(256)S(1)}, u32[]{:S(2)}) copy-start(f32[129]{0:T(256)S(1)} %scatter_custom_fusion.1) | copy-start | bytes 1552
  65.9 5.5 %slice-start = ((f32[129]{0:T(256)}), f32[128]{0:T(128)S(1)}, s32[]{:S(2)}) async-start(f32[129]{0:T(256)} %copy-done.1), calls=%async_computation.4 | async-start | bytes 1024 | tf_op jit(solution)/shard_map/slice | solution.py:32
Sparse Core Ops, SparseCore 0:
  36.3 26.5 all-gather.2
where the time goes:
time: 97.8 us; the launch traced here: 97.4 us
  blocking collectives  48.7 us (50%)
  other arithmetic  13.7 us (14%)
  between operations  13.5 us (14%)
  waiting for transfers between devices  11.8 us (12%)
  starting transfers between devices  3.94 us (4%)
  matrix products  3.43 us (4%)
  local copies, waits for them, and re-layouts  2.3 us (2%)
    all_to_all x1, blocking collectives, on_device(): lax.all_to_all(outgoing.reshape(owners_count, capacity, width), 'rows', s...  27.4 us
    all_to_all x1, blocking collectives, on_device(): lax.all_to_all(slot_score.reshape(owners_count, capacity), 'rows', split_...  11.9 us
    all_to_all x1, waiting for transfers between devices, on_device(): lax.all_to_all(out_ids.reshape(owners_count, capacity), 'rows', split_axi...  6.42 us
    all_gather x1, waiting for transfers between devices, on_device(): portion_rows = lax.all_gather(key_rows, 'split', axis=0, tiled=True)  5.4 us
    psum x1, blocking collectives, on_device(): sum_density, counts = lax.psum((sum_density, counts), 'split')  4.93 us
    all_gather x1, blocking collectives, on_device(): portion_ids = lax.all_gather(key_ids, 'split', axis=0, tiled=True)  4.54 us
    scatter-add x1, other arithmetic, cluster_means(): jax.ops.segment_sum(jnp.where(present, density, 0.0), segment, clusters_a...  4.09 us
    scatter-add x1, other arithmetic, cluster_means(): jax.ops.segment_sum(present.astype(jnp.float32), segment, clusters_all + 1)  4.09 us
  transfers between devices with their start and end apart: 2, of which 2 were waited for; matrix products, arithmetic and copies ran while one was open for 7% of the time, Pallas kernels for 0%

commit v1 on v0

--- a/solution.py
+++ b/solution.py
@@ -75,7 +75,14 @@
         jnp.full((slot_count,), FLOOR_SCORE, jnp.float32),
         jnp.zeros((slot_count,), jnp.float32),
     )
-    portion_rows = lax.all_gather(key_rows, "split", axis=0, tiled=True)
+    ways, here = (lax.axis_size("split"), lax.axis_index("split"))
+    portion_rows, reach = (key_rows, 1)
+    while reach < ways:
+        theirs = lax.ppermute(portion_rows, "split", [(d, d ^ reach) for d in range(ways)])
+        mine_first = jnp.concatenate([portion_rows, theirs], axis=0)
+        theirs_first = jnp.concatenate([theirs, portion_rows], axis=0)
+        portion_rows = jnp.where(here & reach == 0, mine_first, theirs_first)
+        reach = 2 * reach
     portion_ids = lax.all_gather(key_ids, "split", axis=0, tiled=True)
     length = portion_ids.shape[0]
     key_positions = jnp.arange(length, dtype=jnp.int32)

time: 97.8 us -> 82.6 us (0.84)
  blocking collectives: 48.7 us -> 24.9 us
  between operations: 13.5 us -> 0.11 us
  waiting for transfers between devices: 11.8 us -> 22.7 us
  starting transfers between devices: 3.94 us -> 14.3 us
    all_to_all x1 -> x0, blocking collectives: 27.4 us -> none  [on_device(): lax.all_to_all(outgoing.reshape(owners_count, capacity, width), 'rows', s...]
    all_to_all x0 -> x1, waiting for transfers between devices: none -> 17.8 us  [on_device(): lax.all_to_all(outgoing.reshape(owners_count, capacity, width), 'rows', s...]
    all_to_all x0 -> x1, starting transfers between devices: none -> 7.38 us  [on_device(): lax.all_to_all(outgoing.reshape(owners_count, capacity, width), 'rows', s...]
    all_gather x1 -> x0, waiting for transfers between devices: 5.4 us -> none  [on_device(): portion_rows = lax.all_gather(key_rows, 'split', axis=0, tiled=True)]
    all_gather x1, blocking collectives: 4.54 us -> 8.04 us  [on_device(): portion_ids = lax.all_gather(key_ids, 'split', axis=0, tiled=True)]
    ppermute x0 -> x1, starting transfers between devices: none -> 1.58 us  [on_device(): lax.ppermute(portion_rows, 'split', [(d, d ^ reach) for d in range(ways)])]
    all_to_all x1, waiting for transfers between devices: 6.42 us -> 4.85 us  [on_device(): lax.all_to_all(out_ids.reshape(owners_count, capacity), 'rows', split_axi...]
    all_to_all x1, starting transfers between devices: 3.93 us -> 5.38 us  [on_device(): lax.all_to_all(out_ids.reshape(owners_count, capacity), 'rows', split_axi...]
  transfers between devices with their start and end apart: 2 -> 3, of which waited for: 2 -> 2; matrix products, arithmetic and copies ran while one was open for 7% -> 8% of each run, Pallas kernels for 0% -> 0%
where the time goes in v1:
time: 82.6 us; the launch traced here: 82.2 us
  blocking collectives  24.9 us (30%)
  waiting for transfers between devices  22.7 us (27%)
  starting transfers between devices  14.3 us (17%)
  other arithmetic  13.7 us (17%)
  matrix products  4.16 us (5%)
  local copies, waits for them, and re-layouts  2.3 us (3%)
    all_to_all x1, waiting for transfers between devices, on_device(): lax.all_to_all(outgoing.reshape(owners_count, capacity, width), 'rows', s...  17.8 us
    all_to_all x1, blocking collectives, on_device(): lax.all_to_all(slot_score.reshape(owners_count, capacity), 'rows', split_...  12 us
    all_gather x1, blocking collectives, on_device(): portion_ids = lax.all_gather(key_ids, 'split', axis=0, tiled=True)  8.04 us
    all_to_all x1, starting transfers between devices, on_device(): lax.all_to_all(outgoing.reshape(owners_count, capacity, width), 'rows', s...  7.38 us
    all_to_all x1, starting transfers between devices, on_device(): lax.all_to_all(out_ids.reshape(owners_count, capacity), 'rows', split_axi...  5.38 us
    psum x1, blocking collectives, on_device(): sum_density, counts = lax.psum((sum_density, counts), 'split')  4.93 us
    all_to_all x1, waiting for transfers between devices, on_device(): lax.all_to_all(out_ids.reshape(owners_count, capacity), 'rows', split_axi...  4.85 us
    scatter-add x1, other arithmetic, cluster_means(): jax.ops.segment_sum(jnp.where(present, density, 0.0), segment, clusters_a...  4.09 us
  transfers between devices with their start and end apart: 3, of which 2 were waited for; matrix products, arithmetic and copies ran while one was open for 8% of the time, Pallas kernels for 0%

profile of v1, /device:TPU:0, one launch (start us, length us, event | category | flops | bytes accessed | tf_op | source)
XLA Modules:
  0.0 82.2 jit_solution(18114208266629917843)
XLA Ops:
  0.0 0.0 copy-start
  0.0 0.9 %select_reduce_fusion.4 = s32[256]{0:T(256)S(1)} fusion(s32[128]{0:T(128)} %param.5, s32[256]{0:T(256)} %param.4), kind=kLoop, calls=%fused_computation.25 | loop fusion | flops 98048 | bytes 2560 | tf_op jit(solution)/shard_map/reduce_sum | solution.py:47
  0.9 0.2 convert_reduce_fusion
  1.1 0.7 multiply_add_fusion
  1.8 0.0 copy-done
  1.8 1.3 %convolution_convert_fusion = bf16[512,768]{1,0:T(8,128)(2,1)} fusion(bf16[256,768]{1,0:T(8,128)(2,1)S(1)} %copy-done, s32[256]{0:T(256)S(1)} %get-tuple-element.11), kind=kOutput, calls=%fused_computation.15 | convolution fusion | flops 201850880 | bytes 1180672 | tf_op jit(solution)/shard_map/dot_general | solution.py:53
  3.1 7.4 %all-to-all-start.1 = ((bf16[16,32,768]{2,1,0:T(8,128)(2,1)}), bf16[16,32,768]{2,1,0:T(8,128)(2,1)S(1)}, u32[]{:S(2)}, u32[]{:S(2)}) async-start(bf16[16,32,768]{2,1,0:T(8,128)(2,1)} %bitcast.1), calls=%async_computation.1 | async-start | bytes 1572864 | tf_op jit(solution)/shard_map/all_to_all | solution.py:58
  10.5 0.1 select_reduce_fusion.2
  10.6 0.7 sub.39
  11.3 17.8 %all-to-all-done.1 = bf16[16,32,768]{2,1,0:T(8,128)(2,1)S(1)} async-done(((bf16[16,32,768]{2,1,0:T(8,128)(2,1)}), bf16[16,32,768]{2,1,0:T(8,128)(2,1)S(1)}, u32[]{:S(2)}, u32[]{:S(2)}) %all-to-all-start.1) | async-done | bytes 786464 | tf_op jit(solution)/shard_map/all_to_all | solution.py:58
  29.1 5.4 %all-to-all-start = ((s32[16,1,32]{2,1,0:T(1,128)}), s32[16,1,32]{2,1,0:T(1,128)S(1)}, u32[]{:S(2)}, u32[]{:S(2)}) async-start(s32[16,1,32]{2,1,0:T(1,128)} %sub.39), calls=%async_computation | async-start | bytes 16384 | tf_op jit(solution)/shard_map/all_to_all | solution.py:65
  34.5 1.6 %collective-permute-start = (bf16[512,768]{1,0:T(8,128)(2,1)S(1)}, bf16[512,768]{1,0:T(8,128)(2,1)}, u32[]{:S(2)}, u32[]{:S(2)}) collective-permute-start(bf16[512,768]{1,0:T(8,128)(2,1)S(1)} %bitcast.7), channel_id=1, source_target_pairs={{0,1},{1,0},{2,3},{3,2},{4,5},{5,4},{6,7},{7,6},{8,9},{9,8},{10,11... | collective-permute-start | bytes 2359304 | tf_op jit(solution)/shard_map/ppermute | solution.py:81
  36.1 4.8 %all-to-all-done = s32[16,1,32]{2,1,0:T(1,128)S(1)} async-done(((s32[16,1,32]{2,1,0:T(1,128)}), s32[16,1,32]{2,1,0:T(1,128)S(1)}, u32[]{:S(2)}, u32[]{:S(2)}) %all-to-all-start) | async-done | bytes 2080 | tf_op jit(solution)/shard_map/all_to_all | solution.py:65
  41.0 0.1 reshape.127
  41.0 0.1 reshape.130
  41.1 0.5 broadcast.91
  41.6 0.7 reduce.10
  42.3 0.1 reshape.147
  42.4 4.1 %scatter_custom_fusion.1 = f32[129]{0:T(256)S(1)} fusion(s32[512]{0:T(512)S(1)} %bitcast.14, f32[512]{0:T(512)S(1)} %get-tuple-element.7, f32[]{:T(128)} %constant.5.clone.1), kind=kCustom, calls=%fused_computation.46 | custom fusion | flops 512 | bytes 520 | tf_op jit(solution)/shard_map/scatter-add | solution.py:32
  46.5 0.0 copy-start.1
  46.5 8.0 %all-gather = s32[2,1,512]{2,1,0:T(1,128)S(1)} all-gather(s32[1,1,512]{2,1,0:T(1,128)S(1)} %reshape.147), channel_id=1, replica_groups=mesh['rows'=16,'split'=2] {'split'}, dimensions={0}, use_global_device_ids=true | all-gather | bytes 6144 | tf_op jit(solution)/shard_map/all_gather | solution.py:86
  54.5 0.0 collective-permute-done
  54.5 2.9 %fusion.1 = (f32[512]{0:T(512)S(1)}, f32[512,1024]{1,0:T(8,128)S(1)}) fusion(s32[512]{0:T(512)S(1)} %iota_add_fusion, s32[1024]{0:T(1024)S(1)} %bitcast.12, s32[512]{0:T(512)S(1)} %reshape.127, pred[1024]{0:T(1024)(128)(4,1)S(1)} %broadcast_compare_fusion, bf16[512,768]{1,0:T(8,128)(2,1)S(1)} %bitcast.8, bf16[512,768]{1,0:T(8,128)(2,1)} %collective-permute-done, ...), kind=kOutput, calls=%fused_computation.6 | convolution fusion | flops 816053760 | bytes 3681281 | tf_op jit(solution)/shard_map/qd,kd->qk/dot_general | solution.py:12
  57.4 0.0 copy-done.1
  57.5 0.0 slice-start
  57.5 0.1 reduce_max.12
  57.6 1.2 %select_reduce_fusion = f32[512]{0:T(512)S(1)} fusion(f32[512,1024]{1,0:T(8,128)S(1)} %get-tuple-element.10, f32[512]{0:T(512)S(1)} %get-tuple-element.9, s32[512]{0:T(512)S(1)} %iota_add_fusion, s32[1024]{0:T(1024)S(1)} %bitcast.13, s32[512]{0:T(512)S(1)} %reshape.127, pred[1024]{0:T(1024)(128)(4,1)S(1)} %broadcast_compare_fusion), kind=kLoop, calls=%fused_computation.2 | loop fusion | flops 4718080 | bytes 2110464 | tf_op jit(solution)/shard_map/reduce_sum | solution.py:16
  58.7 0.1 reduce_sum.62
  58.8 4.1 %scatter_custom_fusion = f32[129]{0:T(256)S(1)} fusion(s32[512]{0:T(512)S(1)} %bitcast.15, f32[512]{0:T(512)S(1)} %fusion.17, f32[]{:T(128)} %constant.5.clone.1), kind=kCustom, calls=%fused_computation.48 | custom fusion | flops 512 | bytes 520 | tf_op jit(solution)/shard_map/scatter-add | solution.py:29
  62.9 0.0 slice-done
  63.0 4.9 %all-reduce = (f32[128]{0:T(128)S(1)}, f32[128]{0:T(128)S(1)}) all-reduce(f32[128]{0:T(128)S(1)} %slice.6, f32[128]{0:T(128)S(1)} %slice-done), channel_id=1, replica_groups=mesh['rows'=16,'split'=2] {'split'}, use_global_device_ids=true, to_apply=%region_6.7 | all-reduce | flops 256 | bytes 2048 | tf_op jit(solution)/shard_map/psum | solution.py:97
  67.9 0.2 select_reduce_fusion.3
  68.1 0.1 reduce_sum.64
  68.3 12.0 %all_to_all.17 = f32[16,1,32]{2,1,0:T(1,128)S(1)} all-to-all(f32[16,1,32]{2,1,0:T(1,128)S(1)} %compare_select_fusion), channel_id=1, replica_groups=mesh['rows'=16,'split'=2] {'rows'}, dimensions={0} | all-to-all | bytes 4096 | tf_op jit(solution)/shard_map/all_to_all | solution.py:102
  80.2 0.5 broadcast.92
  80.7 0.7 reduce.11
  81.4 0.1 broadcast_in_dim.105
  81.5 0.7 select_reduce_fusion.1
  (9 shorter events, 0.1 us)
Async XLA Ops:
  0.0 1.8 %copy-start = (bf16[256,768]{1,0:T(8,128)(2,1)S(1)}, bf16[256,768]{1,0:T(8,128)(2,1)}, u32[]{:S(2)}) copy-start(bf16[256,768]{1,0:T(8,128)(2,1)} %param.3) | copy-start | bytes 1179652
  3.1 26.1 %all-to-all-start.1 = ((bf16[16,32,768]{2,1,0:T(8,128)(2,1)}), bf16[16,32,768]{2,1,0:T(8,128)(2,1)S(1)}, u32[]{:S(2)}, u32[]{:S(2)}) async-start(bf16[16,32,768]{2,1,0:T(8,128)(2,1)} %bitcast.1), calls=%async_computation.1 | async-start | bytes 1572864 | tf_op jit(solution)/shard_map/all_to_all | solution.py:58
  29.1 11.8 %all-to-all-start = ((s32[16,1,32]{2,1,0:T(1,128)}), s32[16,1,32]{2,1,0:T(1,128)S(1)}, u32[]{:S(2)}, u32[]{:S(2)}) async-start(s32[16,1,32]{2,1,0:T(1,128)} %sub.39), calls=%async_computation | async-start | bytes 16384 | tf_op jit(solution)/shard_map/all_to_all | solution.py:65
  34.5 20.0 %collective-permute-start = (bf16[512,768]{1,0:T(8,128)(2,1)S(1)}, bf16[512,768]{1,0:T(8,128)(2,1)}, u32[]{:S(2)}, u32[]{:S(2)}) collective-permute-start(bf16[512,768]{1,0:T(8,128)(2,1)S(1)} %bitcast.7), channel_id=1, source_target_pairs={{0,1},{1,0},{2,3},{3,2},{4,5},{5,4},{6,7},{7,6},{8,9},{9,8},{10,11... | collective-permute-start | bytes 2359304 | tf_op jit(solution)/shard_map/ppermute | solution.py:81
  46.5 11.0 %copy-start.1 = (f32[129]{0:T(256)}, f32[129]{0:T(256)S(1)}, u32[]{:S(2)}) copy-start(f32[129]{0:T(256)S(1)} %scatter_custom_fusion.1) | copy-start | bytes 1552
  57.5 5.5 %slice-start = ((f32[129]{0:T(256)}), f32[128]{0:T(128)S(1)}, s32[]{:S(2)}) async-start(f32[129]{0:T(256)} %copy-done.1), calls=%async_computation.3 | async-start | bytes 1024 | tf_op jit(solution)/shard_map/slice | solution.py:32
